TPU v7x, 128 devices: a whole 4x4x4 slice. The times are simulated.
128 devices in a mesh: row: 16 (over x, z), col: 8 (over y, core).
Axes of the slice: x: 4, y: 4, z: 4, core: 2. Of those that a mesh axis runs over, the one named last changes fastest.
Arguments:
- t_upper: bfloat16 [3, 4096, 4096], P(None, 'row', 'col'), may hold values from -0.03125 to 0.03125
- t_old: bfloat16 [3, 4096, 24576], P(None, 'row', 'col'), may hold values from -0.03125 to 0.03125
- inverses: bfloat16 [3, 4096, 4096], P(None, 'row', 'col'), may hold values from -1 to 1.5, as said below
- forcing: float32 [3, 4096, 128], P(None, 'row'), may hold values from -6 to 6
- x_old: bfloat16 [24576, 128], P('col'), may hold values from -6 to 6
- offsets: float32 [128], replicated, may hold values from -0.5 to 0.5
- starts: int32 [128], replicated, may hold values from 0 to 36864
- column_map: int32 [128], replicated, may hold values from 0 to 127, each once
- z_cols: bfloat16 [49152, 3, 4096], P('row', None, 'col'), may hold values from -0.0546875 to 0.0546875
- acc: float32 [49152, 128], P(('row', 'col')), may hold values from -6 to 6
Outputs:
- solved: float32 [3, 4096, 128], P(None, ('row', 'col'))
- acc_out: float32 [49152, 128], P(('row', 'col'))
Inputs may be any that keep to these rules, and one draw needn't show every extreme that they name: `inverses`: dense matrices with a dominant positive diagonal.
All inputs are finite; a program needn't handle non-finite values.
Results may differ from a plain program's by a relative error of at most 0.0003.
Values may be sent and summed in bfloat16 or wider, within the bound.
No kernel may reach another device: no remote copies, remote signals or barrier semaphores. Data moves between devices by JAX's collectives and lax.ppermute only.
A program may use at most 128 MiB of HBM per device.

v0:
```python
import jax
import jax.numpy as jnp
from jax import lax
from jax.sharding import PartitionSpec as P

NEUMANN = 3


def split_pair(values):
    upper = values.astype(jnp.bfloat16)
    lower = (values - lax.optimization_barrier(upper).astype(jnp.float32)).astype(jnp.bfloat16)
    return jnp.concatenate([upper, lower], axis=-1)


def body(t_upper, t_old, inverses, forcing, x_old, offsets, starts, column_map, z_cols, acc):
    n_col = lax.axis_size("col")
    row_idx = lax.axis_index("row")
    col_idx = lax.axis_index("col")
    steps = forcing.shape[0]
    row_block = t_upper.shape[1]
    col_block = t_upper.shape[2]
    width = forcing.shape[2]
    old_cols = x_old.shape[0]
    full_rows = col_block * n_col
    share = row_block // n_col
    pairs = {}
    count = 0
    for first in range(steps):
        for second in range(first + 1, steps):
            pairs[first, second] = count
            count = count + 1

    def fold_pair(product):
        return product[:, :width] + product[:, width:]

    old_rows = steps * full_rows + col_idx * old_cols + jnp.arange(old_cols, dtype=jnp.int32)
    old_live = old_rows[:, None] < starts[None, :]
    old_vals = jnp.where(old_live, x_old, jnp.zeros_like(x_old))
    local_start = row_idx * row_block

    def reduce_rows(partial_value):
        return lax.psum(partial_value, "col")

    def spread_rows(values):
        return lax.all_gather(values, "row", axis=0, tiled=True)

    def own_cols(whole):
        return lax.dynamic_slice_in_dim(whole, col_idx * col_block, col_block, 0)

    solved_full = {}
    pieces = {}
    for step in reversed(range(steps)):
        partial_value = -jnp.dot(t_old[step], old_vals, preferred_element_type=jnp.float32)
        for later in range(step + 1, steps):
            partial_value = partial_value - fold_pair(
                jnp.dot(
                    t_upper[pairs[step, later]],
                    own_cols(solved_full[later]),
                    preferred_element_type=jnp.float32,
                )
            )
        rhs = reduce_rows(partial_value) + forcing[step]
        gathered = spread_rows(split_pair(rhs))
        term = reduce_rows(
            fold_pair(
                jnp.dot(inverses[step], own_cols(gathered), preferred_element_type=jnp.float32)
            )
        )
        total = term
        for extra in range(1, NEUMANN):
            gathered = spread_rows(split_pair(term))
            term = (
                reduce_rows(
                    fold_pair(
                        jnp.dot(
                            inverses[step], own_cols(gathered), preferred_element_type=jnp.float32
                        )
                    )
                )
                * offsets[None, :]
            )
            total = total + term
        rows = step * full_rows + local_start + jnp.arange(row_block, dtype=jnp.int32)
        total = jnp.where(rows[:, None] < starts[None, :], total, jnp.zeros_like(total))
        pieces[step] = lax.dynamic_slice_in_dim(total, col_idx * share, share, 0)
        solved_full[step] = spread_rows(split_pair(total))
    stacked = jnp.concatenate([own_cols(solved_full[step]) for step in range(steps)], axis=0)
    one_hot = (jnp.arange(width, dtype=jnp.int32)[:, None] == column_map[None, :]).astype(
        jnp.bfloat16
    )
    picked_upper = jnp.dot(stacked[:, :width], one_hot, preferred_element_type=jnp.float32).astype(
        jnp.bfloat16
    )
    picked_lower = jnp.dot(stacked[:, width:], one_hot, preferred_element_type=jnp.float32).astype(
        jnp.bfloat16
    )
    picked = jnp.concatenate([picked_upper, picked_lower], axis=1)
    z_rows = z_cols.shape[0]
    z_flat = z_cols.reshape(z_rows, steps * col_block)
    contribution = lax.psum_scatter(
        fold_pair(jnp.dot(z_flat, picked, preferred_element_type=jnp.float32)),
        "col",
        scatter_dimension=0,
        tiled=True,
    )
    solved = jnp.stack([pieces[step] for step in range(steps)])
    return (solved, acc + contribution)


def solution(mesh):
    placed = (
        P(None, "row", "col"),
        P(None, "row", "col"),
        P(None, "row", "col"),
        P(None, "row", None),
        P("col", None),
        P(),
        P(),
        P(),
        P("row", None, "col"),
        P(("row", "col"), None),
    )
    return jax.shard_map(
        body,
        mesh=mesh,
        in_specs=placed,
        out_specs=(P(None, ("row", "col"), None), P(("row", "col"), None)),
        check_vma=False,
    )
```

profile of v0, /device:TPU:0, one launch (start us, length us, event | category | flops | bytes accessed | tf_op | source)
XLA Modules:
  0.0 1396.4 jit_solution(2241294068387488249)
XLA Ops:
  11.0 62.4 %all-reduce.13.cloned.1.call-done = f32[256,128]{0,1:T(8,128)} async-done(((f32[256,128]{0,1:T(8,128)}), f32[256,128]{0,1:T(8,128)}) %all-reduce.13.cloned.1.call-update) | async-done | bytes 131088 | tf_op jit(solution)/shard_map/psum | solution.py:42
  76.0 46.2 %all-gather.13.cloned.1.call-done = bf16[4096,256]{0,1:T(8,128)(2,1)} async-done(((bf16[256,256]{0,1:T(8,128)(2,1)}), bf16[4096,256]{0,1:T(8,128)(2,1)}) %all-gather.13.cloned.1.call-update) | async-done | bytes 2097168 | tf_op jit(solution)/shard_map/all_gather | solution.py:45
  124.2 60.2 %all-reduce.15.cloned.1.call-done = f32[256,128]{0,1:T(8,128)} async-done(((f32[256,128]{0,1:T(8,128)}), f32[256,128]{0,1:T(8,128)}) %all-reduce.15.cloned.1.call-update) | async-done | bytes 131088 | tf_op jit(solution)/shard_map/psum | solution.py:42
  187.0 46.2 %all-gather.15.cloned.1.call-done = bf16[4096,256]{0,1:T(8,128)(2,1)} async-done(((bf16[256,256]{0,1:T(8,128)(2,1)}), bf16[4096,256]{0,1:T(8,128)(2,1)}) %all-gather.15.cloned.1.call-update) | async-done | bytes 2097168 | tf_op jit(solution)/shard_map/all_gather | solution.py:45
  235.2 60.1 %all-reduce.17.cloned.1.call-done = f32[256,128]{0,1:T(8,128)} async-done(((f32[256,128]{0,1:T(8,128)}), f32[256,128]{0,1:T(8,128)}) %all-reduce.17.cloned.1.call-update) | async-done | bytes 131088 | tf_op jit(solution)/shard_map/psum | solution.py:42
  298.1 46.2 %all-gather.17.cloned.1.call-done = bf16[4096,256]{0,1:T(8,128)(2,1)} async-done(((bf16[256,256]{0,1:T(8,128)(2,1)}), bf16[4096,256]{0,1:T(8,128)(2,1)}) %all-gather.17.cloned.1.call-update) | async-done | bytes 2097168 | tf_op jit(solution)/shard_map/all_gather | solution.py:45
  346.3 60.2 %all-reduce.19.cloned.1.call-done = f32[256,128]{0,1:T(8,128)} async-done(((f32[256,128]{0,1:T(8,128)}), f32[256,128]{0,1:T(8,128)}) %all-reduce.19.cloned.1.call-update) | async-done | bytes 131088 | tf_op jit(solution)/shard_map/psum | solution.py:42
  408.3 47.0 %all-gather.19.cloned.1.call-done = bf16[4096,256]{0,1:T(8,128)(2,1)} async-done(((bf16[256,256]{0,1:T(8,128)(2,1)}), bf16[4096,256]{0,1:T(8,128)(2,1)}) %all-gather.19.cloned.1.call-update) | async-done | bytes 2097168 | tf_op jit(solution)/shard_map/all_gather | solution.py:45
  460.3 59.3 %all-reduce.21.cloned.1.call-done = f32[256,128]{0,1:T(8,128)} async-done(((f32[256,128]{0,1:T(8,128)}), f32[256,128]{0,1:T(8,128)}) %all-reduce.21.cloned.1.call-update) | async-done | bytes 131088 | tf_op jit(solution)/shard_map/psum | solution.py:42
  522.1 46.2 %all-gather.21.cloned.1.call-done = bf16[4096,256]{0,1:T(8,128)(2,1)} async-done(((bf16[256,256]{0,1:T(8,128)(2,1)}), bf16[4096,256]{0,1:T(8,128)(2,1)}) %all-gather.21.cloned.1.call-update) | async-done | bytes 2097168 | tf_op jit(solution)/shard_map/all_gather | solution.py:45
  570.3 60.2 %all-reduce.23.cloned.1.call-done = f32[256,128]{0,1:T(8,128)} async-done(((f32[256,128]{0,1:T(8,128)}), f32[256,128]{0,1:T(8,128)}) %all-reduce.23.cloned.1.call-update) | async-done | bytes 131088 | tf_op jit(solution)/shard_map/psum | solution.py:42
  633.2 46.2 %all-gather.23.cloned.1.call-done = bf16[4096,256]{0,1:T(8,128)(2,1)} async-done(((bf16[256,256]{0,1:T(8,128)(2,1)}), bf16[4096,256]{0,1:T(8,128)(2,1)}) %all-gather.23.cloned.1.call-update) | async-done | bytes 2097168 | tf_op jit(solution)/shard_map/all_gather | solution.py:45
  681.4 60.2 %all-reduce.25.cloned.1.call-done = f32[256,128]{0,1:T(8,128)} async-done(((f32[256,128]{0,1:T(8,128)}), f32[256,128]{0,1:T(8,128)}) %all-reduce.25.cloned.1.call-update) | async-done | bytes 131088 | tf_op jit(solution)/shard_map/psum | solution.py:42
  744.4 46.2 %all-gather.25.cloned.1.call-done = bf16[4096,256]{0,1:T(8,128)(2,1)} async-done(((bf16[256,256]{0,1:T(8,128)(2,1)}), bf16[4096,256]{0,1:T(8,128)(2,1)}) %all-gather.25.cloned.1.call-update) | async-done | bytes 2097168 | tf_op jit(solution)/shard_map/all_gather | solution.py:45
  792.6 60.1 %all-reduce.27.cloned.1.call-done = f32[256,128]{0,1:T(8,128)} async-done(((f32[256,128]{0,1:T(8,128)}), f32[256,128]{0,1:T(8,128)}) %all-reduce.27.cloned.1.call-update) | async-done | bytes 131088 | tf_op jit(solution)/shard_map/psum | solution.py:42
  854.7 46.6 %all-gather.27.cloned.1.call-done = bf16[4096,256]{0,1:T(8,128)(2,1)} async-done(((bf16[256,256]{0,1:T(8,128)(2,1)}), bf16[4096,256]{0,1:T(8,128)(2,1)}) %all-gather.27.cloned.1.call-update) | async-done | bytes 2097168 | tf_op jit(solution)/shard_map/all_gather | solution.py:45
  906.3 59.3 %all-reduce.29.cloned.1.call-done = f32[256,128]{0,1:T(8,128)} async-done(((f32[256,128]{0,1:T(8,128)}), f32[256,128]{0,1:T(8,128)}) %all-reduce.29.cloned.1.call-update) | async-done | bytes 131088 | tf_op jit(solution)/shard_map/psum | solution.py:42
  968.1 46.2 %all-gather.29.cloned.1.call-done = bf16[4096,256]{0,1:T(8,128)(2,1)} async-done(((bf16[256,256]{0,1:T(8,128)(2,1)}), bf16[4096,256]{0,1:T(8,128)(2,1)}) %all-gather.29.cloned.1.call-update) | async-done | bytes 2097168 | tf_op jit(solution)/shard_map/all_gather | solution.py:45
  1016.3 60.2 %all-reduce.31.cloned.1.call-done = f32[256,128]{0,1:T(8,128)} async-done(((f32[256,128]{0,1:T(8,128)}), f32[256,128]{0,1:T(8,128)}) %all-reduce.31.cloned.1.call-update) | async-done | bytes 131088 | tf_op jit(solution)/shard_map/psum | solution.py:42
  1079.2 46.2 %all-gather.31.cloned.1.call-done = bf16[4096,256]{0,1:T(8,128)(2,1)} async-done(((bf16[256,256]{0,1:T(8,128)(2,1)}), bf16[4096,256]{0,1:T(8,128)(2,1)}) %all-gather.31.cloned.1.call-update) | async-done | bytes 2097168 | tf_op jit(solution)/shard_map/all_gather | solution.py:45
  1127.3 60.2 %all-reduce.33.cloned.1.call-done = f32[256,128]{0,1:T(8,128)} async-done(((f32[256,128]{0,1:T(8,128)}), f32[256,128]{0,1:T(8,128)}) %all-reduce.33.cloned.1.call-update) | async-done | bytes 131088 | tf_op jit(solution)/shard_map/psum | solution.py:42
  1190.4 46.2 %all-gather.33.cloned.1.call-done = bf16[4096,256]{0,1:T(8,128)(2,1)} async-done(((bf16[256,256]{0,1:T(8,128)(2,1)}), bf16[4096,256]{0,1:T(8,128)(2,1)}) %all-gather.33.cloned.1.call-update) | async-done | bytes 2097168 | tf_op jit(solution)/shard_map/all_gather | solution.py:45
  1238.6 60.2 %all-reduce.35.cloned.1.call-done = f32[256,128]{0,1:T(8,128)} async-done(((f32[256,128]{0,1:T(8,128)}), f32[256,128]{0,1:T(8,128)}) %all-reduce.35.cloned.1.call-update) | async-done | bytes 131088 | tf_op jit(solution)/shard_map/psum | solution.py:42
  1313.2 34.3 %all-gather.35.cloned.1.call-done = bf16[4096,256]{0,1:T(8,128)(2,1)} async-done(((bf16[256,256]{0,1:T(8,128)(2,1)}), bf16[4096,256]{0,1:T(8,128)(2,1)}) %all-gather.35.cloned.1.call-update) | async-done | bytes 2097168 | tf_op jit(solution)/shard_map/all_gather | solution.py:45
  (164 shorter events, 115.4 us)
Async XLA Ops:
  10.8 111.4 %all-gather.13.cloned.1.call-start = ((), (), s32[]{:S(2)}) async-start(), calls=%async_computation.2 | async-start | bytes 2228224 | tf_op jit(solution)/shard_map/all_gather | solution.py:45
  75.9 108.5 %all-reduce.15.cloned.1.call-start = ((), (), s32[]{:S(2)}) async-start(), calls=%async_computation.3 | async-start | bytes 262144 | tf_op jit(solution)/shard_map/psum | solution.py:42
  124.1 109.1 %all-gather.15.cloned.1.call-start = ((), (), s32[]{:S(2)}) async-start(), calls=%async_computation.4 | async-start | bytes 2228224 | tf_op jit(solution)/shard_map/all_gather | solution.py:45
  187.0 108.3 %all-reduce.17.cloned.1.call-start = ((), (), s32[]{:S(2)}) async-start(), calls=%async_computation.5 | async-start | bytes 262144 | tf_op jit(solution)/shard_map/psum | solution.py:42
  235.2 109.1 %all-gather.17.cloned.1.call-start = ((), (), s32[]{:S(2)}) async-start(), calls=%async_computation.6 | async-start | bytes 2228224 | tf_op jit(solution)/shard_map/all_gather | solution.py:45
  298.1 108.4 %all-reduce.19.cloned.1.call-start = ((), (), s32[]{:S(2)}) async-start(), calls=%async_computation.7 | async-start | bytes 262144 | tf_op jit(solution)/shard_map/psum | solution.py:42
  346.2 109.1 %all-gather.19.cloned.1.call-start = ((), (), s32[]{:S(2)}) async-start(), calls=%async_computation.8 | async-start | bytes 2228224 | tf_op jit(solution)/shard_map/all_gather | solution.py:45
  408.2 111.3 %all-reduce.21.cloned.1.call-start = ((), (), s32[]{:S(2)}) async-start(), calls=%async_computation.9 | async-start | bytes 262144 | tf_op jit(solution)/shard_map/psum | solution.py:42
  460.1 108.2 %all-gather.21.cloned.1.call-start = ((), (), s32[]{:S(2)}) async-start(), calls=%async_computation.10 | async-start | bytes 2228224 | tf_op jit(solution)/shard_map/all_gather | solution.py:45
  522.1 108.5 %all-reduce.23.cloned.1.call-start = ((), (), s32[]{:S(2)}) async-start(), calls=%async_computation.11 | async-start | bytes 262144 | tf_op jit(solution)/shard_map/psum | solution.py:42
  570.3 109.1 %all-gather.23.cloned.1.call-start = ((), (), s32[]{:S(2)}) async-start(), calls=%async_computation.12 | async-start | bytes 2228224 | tf_op jit(solution)/shard_map/all_gather | solution.py:45
  633.1 108.4 %all-reduce.25.cloned.1.call-start = ((), (), s32[]{:S(2)}) async-start(), calls=%async_computation.13 | async-start | bytes 262144 | tf_op jit(solution)/shard_map/psum | solution.py:42
  681.3 109.3 %all-gather.25.cloned.1.call-start = ((), (), s32[]{:S(2)}) async-start(), calls=%async_computation.14 | async-start | bytes 2228224 | tf_op jit(solution)/shard_map/all_gather | solution.py:45
  744.3 108.3 %all-reduce.27.cloned.1.call-start = ((), (), s32[]{:S(2)}) async-start(), calls=%async_computation.15 | async-start | bytes 262144 | tf_op jit(solution)/shard_map/psum | solution.py:42
  792.5 108.8 %all-gather.27.cloned.1.call-start = ((), (), s32[]{:S(2)}) async-start(), calls=%async_computation.16 | async-start | bytes 2228224 | tf_op jit(solution)/shard_map/all_gather | solution.py:45
  854.4 111.2 %all-reduce.29.cloned.1.call-start = ((), (), s32[]{:S(2)}) async-start(), calls=%async_computation.17 | async-start | bytes 262144 | tf_op jit(solution)/shard_map/psum | solution.py:42
  906.1 108.2 %all-gather.29.cloned.1.call-start = ((), (), s32[]{:S(2)}) async-start(), calls=%async_computation.18 | async-start | bytes 2228224 | tf_op jit(solution)/shard_map/all_gather | solution.py:45
  968.1 108.4 %all-reduce.31.cloned.1.call-start = ((), (), s32[]{:S(2)}) async-start(), calls=%async_computation.19 | async-start | bytes 262144 | tf_op jit(solution)/shard_map/psum | solution.py:42
  1016.2 109.1 %all-gather.31.cloned.1.call-start = ((), (), s32[]{:S(2)}) async-start(), calls=%async_computation.20 | async-start | bytes 2228224 | tf_op jit(solution)/shard_map/all_gather | solution.py:45
  1079.1 108.5 %all-reduce.33.cloned.1.call-start = ((), (), s32[]{:S(2)}) async-start(), calls=%async_computation.21 | async-start | bytes 262144 | tf_op jit(solution)/shard_map/psum | solution.py:42
  1127.3 109.3 %all-gather.33.cloned.1.call-start = ((), (), s32[]{:S(2)}) async-start(), calls=%async_computation.22 | async-start | bytes 2228224 | tf_op jit(solution)/shard_map/all_gather | solution.py:45
  1190.3 108.5 %all-reduce.35.cloned.1.call-start = ((), (), s32[]{:S(2)}) async-start(), calls=%async_computation.23 | async-start | bytes 262144 | tf_op jit(solution)/shard_map/psum | solution.py:42
  1238.5 109.0 %all-gather.35.cloned.1.call-start = ((), (), s32[]{:S(2)}) async-start(), calls=%async_computation.24 | async-start | bytes 2228224 | tf_op jit(solution)/shard_map/all_gather | solution.py:45
  1300.5 87.6 %reduce-scatter.2.cloned.1.call-start = ((), (), s32[]{:S(2)}) async-start(), calls=%async_computation.25 | async-start | bytes 1769472 | tf_op jit(solution)/shard_map/reduce_scatter | solution.py:100
  (14 other events, 1878.5 us)
Sparse Core Ops, SparseCore 0:
  11.0 62.3 all-reduce.12
  76.1 46.0 all-gather.12
  125.1 59.2 all-reduce.14
  187.1 46.0 all-gather.14
  236.0 59.2 all-reduce.16
  298.2 46.0 all-gather.16
  347.2 59.2 all-reduce.18
  409.2 46.0 all-gather.18
  460.2 59.2 all-reduce.20
  522.2 46.0 all-gather.20
  571.2 59.2 all-reduce.22
  633.3 46.0 all-gather.22
  682.3 59.2 all-reduce.24
  744.4 46.0 all-gather.24
  793.3 59.2 all-reduce.26
  855.2 46.0 all-gather.26
  906.2 59.2 all-reduce.28
  968.2 46.0 all-gather.28
  1017.2 59.2 all-reduce.30
  1079.2 46.0 all-gather.30
  1128.3 59.2 all-reduce.32
  1190.4 46.0 all-gather.32
  1239.5 59.2 all-reduce.34
  1301.3 46.0 all-gather.34
  (1 shorter events, 32.2 us)
where the time goes:
time: 1400 us
  waiting for transfers between devices  1300 us (93%)
  other arithmetic  37.5 us (3%)
  matrix products  28.1 us (2%)
  local copies, waits for them, and re-layouts  17.3 us (1%)
  between operations  14.6 us (1%)
    psum x12, waiting for transfers between devices, reduce_rows(): return lax.psum(partial_value, 'col')  723 us
    all_gather x12, waiting for transfers between devices, spread_rows(): return lax.all_gather(values, 'row', axis=0, tiled=True)  544 us
    reduce_scatter x1, waiting for transfers between devices, body(): lax.psum_scatter(fold_pair(jnp.dot(z_flat, picked, preferred_element_type...  31.1 us
  transfers between devices with their start and end apart: 25, of which 25 were waited for; matrix products, arithmetic and copies ran while one was open for 1% of the time, Pallas kernels for 0%

commit v1 on v0

--- a/solution.py
+++ b/solution.py
@@ -4,6 +4,13 @@
 from jax.sharding import PartitionSpec as P
 
 NEUMANN = 3
+
+
+def all_by_exchange(x, axis, dim):
+    n_dev = lax.axis_size(axis)
+    blocks = jnp.stack([x for _ in range(n_dev)])
+    blocks = lax.all_to_all(blocks, axis, split_axis=0, concat_axis=0)
+    return jnp.concatenate(blocks, axis=dim)
 
 
 def split_pair(values):
@@ -42,7 +49,7 @@
         return lax.psum(partial_value, "col")
 
     def spread_rows(values):
-        return lax.all_gather(values, "row", axis=0, tiled=True)
+        return all_by_exchange(values, "row", 0)
 
     def own_cols(whole):
         return lax.dynamic_slice_in_dim(whole, col_idx * col_block, col_block, 0)

time: 1400 us -> 1230 us (0.88)
  waiting for transfers between devices: 1300 us -> 867 us
  blocking collectives: 0 us -> 230 us
  starting transfers between devices: 1.04 us -> 35.7 us
    all_gather x12 -> x0, waiting for transfers between devices: 544 us -> none  [spread_rows(): return lax.all_gather(values, 'row', axis=0, tiled=True)]
    all_to_all x0 -> x7, blocking collectives: none -> 230 us  [all_by_exchange(): blocks = lax.all_to_all(blocks, axis, split_axis=0, concat_axis=0)]
    all_to_all x0 -> x5, waiting for transfers between devices: none -> 124 us  [all_by_exchange(): blocks = lax.all_to_all(blocks, axis, split_axis=0, concat_axis=0)]
    all_to_all x0 -> x5, starting transfers between devices: none -> 35.1 us  [all_by_exchange(): blocks = lax.all_to_all(blocks, axis, split_axis=0, concat_axis=0)]
  transfers between devices with their start and end apart: 25 -> 18, of which waited for: 25 -> 18; matrix products, arithmetic and copies ran while one was open for 1% -> 1% of each run, Pallas kernels for 0% -> 0%
where the time goes in v1:
time: 1230 us
  waiting for transfers between devices  867 us (70%)
  blocking collectives  230 us (19%)
  starting transfers between devices  35.7 us (3%)
  other arithmetic  29.2 us (2%)
  local copies, waits for them, and re-layouts  26.5 us (2%)
  matrix products  23.5 us (2%)
  between operations  14.6 us (1%)
    psum x12, waiting for transfers between devices, reduce_rows(): return lax.psum(partial_value, 'col')  711 us
    all_to_all x7, blocking collectives, all_by_exchange(): blocks = lax.all_to_all(blocks, axis, split_axis=0, concat_axis=0)  230 us
    all_to_all x5, waiting for transfers between devices, all_by_exchange(): blocks = lax.all_to_all(blocks, axis, split_axis=0, concat_axis=0)  124 us
    all_to_all x5, starting transfers between devices, all_by_exchange(): blocks = lax.all_to_all(blocks, axis, split_axis=0, concat_axis=0)  35.1 us
    reduce_scatter x1, waiting for transfers between devices, body(): lax.psum_scatter(fold_pair(jnp.dot(z_flat, picked, preferred_element_type...  31.6 us
  transfers between devices with their start and end apart: 18, of which 18 were waited for; matrix products, arithmetic and copies ran while one was open for 1% of the time, Pallas kernels for 0%

profile of v1, /device:TPU:0, one launch (start us, length us, event | category | flops | bytes accessed | tf_op | source)
XLA Modules:
  0.0 1227.1 jit_solution(8008030036907660119)
XLA Ops:
  11.6 61.9 %all-reduce.13.cloned.1.call-done = f32[256,128]{0,1:T(8,128)} async-done(((f32[256,128]{0,1:T(8,128)}), f32[256,128]{0,1:T(8,128)}) %all-reduce.13.cloned.1.call-update) | async-done | bytes 131088 | tf_op jit(solution)/shard_map/psum | solution.py:49
  84.1 27.7 %all-to-all-done = bf16[16,256,256]{2,1,0:T(8,128)(2,1)S(1)} async-done(((bf16[16,256,256]{2,1,0:T(8,128)(2,1)}), bf16[16,256,256]{2,1,0:T(8,128)(2,1)S(1)}, u32[]{:S(2)}, u32[]{:S(2)}) %all-to-all-start) | async-done | bytes 2097184 | tf_op jit(solution)/shard_map/all_to_all | solution.py:12
  112.9 60.2 %all-reduce.15.cloned.1.call-done = f32[256,128]{0,1:T(8,128)} async-done(((f32[256,128]{0,1:T(8,128)}), f32[256,128]{0,1:T(8,128)}) %all-reduce.15.cloned.1.call-update) | async-done | bytes 131088 | tf_op jit(solution)/shard_map/psum | solution.py:49
  175.3 32.9 %all_to_all.60 = bf16[16,256,256]{2,1,0:T(8,128)(2,1)S(1)} all-to-all(bf16[16,256,256]{2,1,0:T(8,128)(2,1)S(1)} %stack.33), channel_id=1, replica_groups=mesh['row'=16,'col'=8] {'row'}, dimensions={0} | all-to-all | bytes 4194304 | tf_op jit(solution)/shard_map/all_to_all | solution.py:12
  209.1 58.5 %all-reduce.17.cloned.1.call-done = f32[256,128]{0,1:T(8,128)} async-done(((f32[256,128]{0,1:T(8,128)}), f32[256,128]{0,1:T(8,128)}) %all-reduce.17.cloned.1.call-update) | async-done | bytes 131088 | tf_op jit(solution)/shard_map/psum | solution.py:49
  278.4 27.7 %all-to-all-done.2 = bf16[16,256,256]{2,1,0:T(8,128)(2,1)S(1)} async-done(((bf16[16,256,256]{2,1,0:T(8,128)(2,1)}), bf16[16,256,256]{2,1,0:T(8,128)(2,1)S(1)}, u32[]{:S(2)}, u32[]{:S(2)}) %all-to-all-start.2) | async-done | bytes 2097184 | tf_op jit(solution)/shard_map/all_to_all | solution.py:12
  307.1 60.2 %all-reduce.19.cloned.1.call-done = f32[256,128]{0,1:T(8,128)} async-done(((f32[256,128]{0,1:T(8,128)}), f32[256,128]{0,1:T(8,128)}) %all-reduce.19.cloned.1.call-update) | async-done | bytes 131088 | tf_op jit(solution)/shard_map/psum | solution.py:49
  368.7 33.0 %all_to_all.61 = bf16[16,256,256]{2,1,0:T(8,128)(2,1)S(1)} all-to-all(bf16[16,256,256]{2,1,0:T(8,128)(2,1)S(1)} %stack.35), channel_id=1, replica_groups=mesh['row'=16,'col'=8] {'row'}, dimensions={0} | all-to-all | bytes 4194304 | tf_op jit(solution)/shard_map/all_to_all | solution.py:12
  406.9 58.3 %all-reduce.21.cloned.1.call-done = f32[256,128]{0,1:T(8,128)} async-done(((f32[256,128]{0,1:T(8,128)}), f32[256,128]{0,1:T(8,128)}) %all-reduce.21.cloned.1.call-update) | async-done | bytes 131088 | tf_op jit(solution)/shard_map/psum | solution.py:49
  467.3 32.9 %all_to_all.62 = bf16[16,256,256]{2,1,0:T(8,128)(2,1)S(1)} all-to-all(bf16[16,256,256]{2,1,0:T(8,128)(2,1)S(1)} %stack.36), channel_id=1, replica_groups=mesh['row'=16,'col'=8] {'row'}, dimensions={0} | all-to-all | bytes 4194304 | tf_op jit(solution)/shard_map/all_to_all | solution.py:12
  501.2 58.4 %all-reduce.23.cloned.1.call-done = f32[256,128]{0,1:T(8,128)} async-done(((f32[256,128]{0,1:T(8,128)}), f32[256,128]{0,1:T(8,128)}) %all-reduce.23.cloned.1.call-update) | async-done | bytes 131088 | tf_op jit(solution)/shard_map/psum | solution.py:49
  561.8 32.9 %all_to_all.63 = bf16[16,256,256]{2,1,0:T(8,128)(2,1)S(1)} all-to-all(bf16[16,256,256]{2,1,0:T(8,128)(2,1)S(1)} %stack.37), channel_id=1, replica_groups=mesh['row'=16,'col'=8] {'row'}, dimensions={0} | all-to-all | bytes 4194304 | tf_op jit(solution)/shard_map/all_to_all | solution.py:12
  595.7 58.5 %all-reduce.25.cloned.1.call-done = f32[256,128]{0,1:T(8,128)} async-done(((f32[256,128]{0,1:T(8,128)}), f32[256,128]{0,1:T(8,128)}) %all-reduce.25.cloned.1.call-update) | async-done | bytes 131088 | tf_op jit(solution)/shard_map/psum | solution.py:49
  664.9 27.7 %all-to-all-done.6 = bf16[16,256,256]{2,1,0:T(8,128)(2,1)S(1)} async-done(((bf16[16,256,256]{2,1,0:T(8,128)(2,1)}), bf16[16,256,256]{2,1,0:T(8,128)(2,1)S(1)}, u32[]{:S(2)}, u32[]{:S(2)}) %all-to-all-start.6) | async-done | bytes 2097184 | tf_op jit(solution)/shard_map/all_to_all | solution.py:12
  693.6 60.2 %all-reduce.27.cloned.1.call-done = f32[256,128]{0,1:T(8,128)} async-done(((f32[256,128]{0,1:T(8,128)}), f32[256,128]{0,1:T(8,128)}) %all-reduce.27.cloned.1.call-update) | async-done | bytes 131088 | tf_op jit(solution)/shard_map/psum | solution.py:49
  766.2 25.8 %all-to-all-done.7 = bf16[16,256,256]{2,1,0:T(8,128)(2,1)S(1)} async-done(((bf16[16,256,256]{2,1,0:T(8,128)(2,1)}), bf16[16,256,256]{2,1,0:T(8,128)(2,1)S(1)}, u32[]{:S(2)}, u32[]{:S(2)}) %all-to-all-start.7) | async-done | bytes 2097184 | tf_op jit(solution)/shard_map/all_to_all | solution.py:12
  797.0 60.1 %all-reduce.29.cloned.1.call-done = f32[256,128]{0,1:T(8,128)} async-done(((f32[256,128]{0,1:T(8,128)}), f32[256,128]{0,1:T(8,128)}) %all-reduce.29.cloned.1.call-update) | async-done | bytes 131088 | tf_op jit(solution)/shard_map/psum | solution.py:49
  859.3 32.9 %all_to_all.64 = bf16[16,256,256]{2,1,0:T(8,128)(2,1)S(1)} all-to-all(bf16[16,256,256]{2,1,0:T(8,128)(2,1)S(1)} %stack.40), channel_id=1, replica_groups=mesh['row'=16,'col'=8] {'row'}, dimensions={0} | all-to-all | bytes 4194304 | tf_op jit(solution)/shard_map/all_to_all | solution.py:12
  893.2 58.4 %all-reduce.31.cloned.1.call-done = f32[256,128]{0,1:T(8,128)} async-done(((f32[256,128]{0,1:T(8,128)}), f32[256,128]{0,1:T(8,128)}) %all-reduce.31.cloned.1.call-update) | async-done | bytes 131088 | tf_op jit(solution)/shard_map/psum | solution.py:49
  953.7 32.9 %all_to_all.65 = bf16[16,256,256]{2,1,0:T(8,128)(2,1)S(1)} all-to-all(bf16[16,256,256]{2,1,0:T(8,128)(2,1)S(1)} %stack.41), channel_id=1, replica_groups=mesh['row'=16,'col'=8] {'row'}, dimensions={0} | all-to-all | bytes 4194304 | tf_op jit(solution)/shard_map/all_to_all | solution.py:12
  987.6 58.4 %all-reduce.33.cloned.1.call-done = f32[256,128]{0,1:T(8,128)} async-done(((f32[256,128]{0,1:T(8,128)}), f32[256,128]{0,1:T(8,128)}) %all-reduce.33.cloned.1.call-update) | async-done | bytes 131088 | tf_op jit(solution)/shard_map/psum | solution.py:49
  1048.4 33.0 %all_to_all.66 = bf16[16,256,256]{2,1,0:T(8,128)(2,1)S(1)} all-to-all(bf16[16,256,256]{2,1,0:T(8,128)(2,1)S(1)} %stack.42), channel_id=1, replica_groups=mesh['row'=16,'col'=8] {'row'}, dimensions={0} | all-to-all | bytes 4194304 | tf_op jit(solution)/shard_map/all_to_all | solution.py:12
  1082.4 58.4 %all-reduce.35.cloned.1.call-done = f32[256,128]{0,1:T(8,128)} async-done(((f32[256,128]{0,1:T(8,128)}), f32[256,128]{0,1:T(8,128)}) %all-reduce.35.cloned.1.call-update) | async-done | bytes 131088 | tf_op jit(solution)/shard_map/psum | solution.py:49
  1187.2 31.6 %reduce-scatter.2.cloned.1.call-done = f32[384,128]{0,1:T(8,128)} async-done(((f32[3072,128]{0,1:T(8,128)}), f32[384,128]{0,1:T(8,128)}) %reduce-scatter.2.cloned.1.call-update) | async-done | bytes 196624 | tf_op jit(solution)/shard_map/reduce_scatter | solution.py:107
  (180 shorter events, 130.1 us)
Async XLA Ops:
  7.2 66.3 %all-reduce.13.cloned.1.call-start = ((), (), s32[]{:S(2)}) async-start(), calls=%async_computation.13 | async-start | bytes 262144 | tf_op jit(solution)/shard_map/psum | solution.py:49
  77.0 34.9 %all-to-all-start = ((bf16[16,256,256]{2,1,0:T(8,128)(2,1)}), bf16[16,256,256]{2,1,0:T(8,128)(2,1)S(1)}, u32[]{:S(2)}, u32[]{:S(2)}) async-start(bf16[16,256,256]{2,1,0:T(8,128)(2,1)} %stack.32), calls=%async_computation | async-start | bytes 4194304 | tf_op jit(solution)/shard_map/all_to_all | solution.py:12
  84.1 89.0 %all-reduce.15.cloned.1.call-start = ((), (), s32[]{:S(2)}) async-start(), calls=%async_computation.14 | async-start | bytes 262144 | tf_op jit(solution)/shard_map/psum | solution.py:49
  112.9 154.7 %all-reduce.17.cloned.1.call-start = ((), (), s32[]{:S(2)}) async-start(), calls=%async_computation.15 | async-start | bytes 262144 | tf_op jit(solution)/shard_map/psum | solution.py:49
  271.2 96.1 %copy-start.1 = (f32[256,128]{0,1:T(8,128)S(1)}, f32[256,128]{0,1:T(8,128)}, u32[]{:S(2)}) copy-start(f32[256,128]{0,1:T(8,128)} %all-reduce.15.cloned.1.call-done) | copy-start | bytes 393220
  271.2 96.1 %copy-start.4 = (f32[256,128]{0,1:T(8,128)S(1)}, f32[256,128]{0,1:T(8,128)}, u32[]{:S(2)}) copy-start(f32[256,128]{0,1:T(8,128)} %all-reduce.17.cloned.1.call-done) | copy-start | bytes 393220
  271.2 96.1 %copy-start.15 = (s32[128]{0:T(128)S(1)}, s32[128]{0:T(128)}, u32[]{:S(2)}) copy-start(s32[128]{0:T(128)} %param.16) | copy-start | bytes 1540
  271.2 34.9 %all-to-all-start.2 = ((bf16[16,256,256]{2,1,0:T(8,128)(2,1)}), bf16[16,256,256]{2,1,0:T(8,128)(2,1)S(1)}, u32[]{:S(2)}, u32[]{:S(2)}) async-start(bf16[16,256,256]{2,1,0:T(8,128)(2,1)} %stack.34), calls=%async_computation.2 | async-start | bytes 4194304 | tf_op jit(solution)/shard_map/all_to_all | solution.py:12
  278.3 89.0 %all-reduce.19.cloned.1.call-start = ((), (), s32[]{:S(2)}) async-start(), calls=%async_computation.16 | async-start | bytes 262144 | tf_op jit(solution)/shard_map/psum | solution.py:49
  307.1 158.1 %all-reduce.21.cloned.1.call-start = ((), (), s32[]{:S(2)}) async-start(), calls=%async_computation.17 | async-start | bytes 262144 | tf_op jit(solution)/shard_map/psum | solution.py:49
  406.7 152.9 %all-reduce.23.cloned.1.call-start = ((), (), s32[]{:S(2)}) async-start(), calls=%async_computation.18 | async-start | bytes 262144 | tf_op jit(solution)/shard_map/psum | solution.py:49
  501.2 152.9 %all-reduce.25.cloned.1.call-start = ((), (), s32[]{:S(2)}) async-start(), calls=%async_computation.19 | async-start | bytes 262144 | tf_op jit(solution)/shard_map/psum | solution.py:49
  657.8 96.1 %copy-start.2 = (f32[256,128]{0,1:T(8,128)S(1)}, f32[256,128]{0,1:T(8,128)}, u32[]{:S(2)}) copy-start(f32[256,128]{0,1:T(8,128)} %all-reduce.23.cloned.1.call-done) | copy-start | bytes 393220
  657.8 96.1 %copy-start.5 = (f32[256,128]{0,1:T(8,128)S(1)}, f32[256,128]{0,1:T(8,128)}, u32[]{:S(2)}) copy-start(f32[256,128]{0,1:T(8,128)} %all-reduce.25.cloned.1.call-done) | copy-start | bytes 393220
  657.8 34.9 %all-to-all-start.6 = ((bf16[16,256,256]{2,1,0:T(8,128)(2,1)}), bf16[16,256,256]{2,1,0:T(8,128)(2,1)S(1)}, u32[]{:S(2)}, u32[]{:S(2)}) async-start(bf16[16,256,256]{2,1,0:T(8,128)(2,1)} %stack.38), calls=%async_computation.6 | async-start | bytes 4194304 | tf_op jit(solution)/shard_map/all_to_all | solution.py:12
  664.9 89.0 %all-reduce.27.cloned.1.call-start = ((), (), s32[]{:S(2)}) async-start(), calls=%async_computation.20 | async-start | bytes 262144 | tf_op jit(solution)/shard_map/psum | solution.py:49
  757.2 34.7 %all-to-all-start.7 = ((bf16[16,256,256]{2,1,0:T(8,128)(2,1)}), bf16[16,256,256]{2,1,0:T(8,128)(2,1)S(1)}, u32[]{:S(2)}, u32[]{:S(2)}) async-start(bf16[16,256,256]{2,1,0:T(8,128)(2,1)} %stack.39), calls=%async_computation.7 | async-start | bytes 4194304 | tf_op jit(solution)/shard_map/all_to_all | solution.py:12
  764.2 92.9 %all-reduce.29.cloned.1.call-start = ((), (), s32[]{:S(2)}) async-start(), calls=%async_computation.21 | async-start | bytes 262144 | tf_op jit(solution)/shard_map/psum | solution.py:49
  796.9 154.7 %all-reduce.31.cloned.1.call-start = ((), (), s32[]{:S(2)}) async-start(), calls=%async_computation.22 | async-start | bytes 262144 | tf_op jit(solution)/shard_map/psum | solution.py:49
  893.1 152.9 %all-reduce.33.cloned.1.call-start = ((), (), s32[]{:S(2)}) async-start(), calls=%async_computation.23 | async-start | bytes 262144 | tf_op jit(solution)/shard_map/psum | solution.py:49
  987.6 153.2 %all-reduce.35.cloned.1.call-start = ((), (), s32[]{:S(2)}) async-start(), calls=%async_computation.24 | async-start | bytes 262144 | tf_op jit(solution)/shard_map/psum | solution.py:49
  1048.4 92.5 %copy-start.3 = (f32[256,128]{0,1:T(8,128)S(1)}, f32[256,128]{0,1:T(8,128)}, u32[]{:S(2)}) copy-start(f32[256,128]{0,1:T(8,128)} %all-reduce.31.cloned.1.call-done) | copy-start | bytes 393220
  1143.5 34.7 %all-to-all-start.11 = ((bf16[16,256,256]{2,1,0:T(8,128)(2,1)}), bf16[16,256,256]{2,1,0:T(8,128)(2,1)S(1)}, u32[]{:S(2)}, u32[]{:S(2)}) async-start(bf16[16,256,256]{2,1,0:T(8,128)(2,1)} %stack.47), calls=%async_computation.11 | async-start | bytes 4194304 | tf_op jit(solution)/shard_map/all_to_all | solution.py:12
  1150.5 68.3 %reduce-scatter.2.cloned.1.call-start = ((), (), s32[]{:S(2)}) async-start(), calls=%async_computation.25 | async-start | bytes 1769472 | tf_op jit(solution)/shard_map/reduce_scatter | solution.py:107
  (13 other events, 375.1 us)
Sparse Core Ops, SparseCore 0:
  10.9 62.4 all-reduce.12
  113.0 60.0 all-reduce.14
  209.2 58.2 all-reduce.16
  307.2 60.0 all-reduce.18
  406.8 58.2 all-reduce.20
  501.3 58.2 all-reduce.22
  595.8 58.2 all-reduce.24
  693.7 60.0 all-reduce.26
  797.0 60.0 all-reduce.28
  893.2 58.2 all-reduce.30
  987.7 58.2 all-reduce.32
  1082.5 58.2 all-reduce.34
  1185.6 33.1 reduce-scatter.1
